TPU v7x, 32 devices: a whole 2x2x4 slice. The times are simulated.
32 devices in a mesh: subj: 2 (over x), row: 8 (over z, y), col: 2 (over core).
Axes of the slice: x: 2, y: 2, z: 4, core: 2. Of those that a mesh axis runs over, the one named last changes fastest.
Arguments:
- series: float32 [256, 11392], P(('subj', 'row', 'col')), parts along dimension 0, may hold values from -30 to 30
- tap_values: float32 [17], replicated, may hold values from -4 to 4
- tap_count: int32 [1], replicated, may hold values from 4 to 8
- kept_frames: int32 [32], P('subj'), parts along dimension 0, may hold values from 1 to 8, 96 in all
- band_start: int32 [2], P('subj'), parts along dimension 0, may hold values from 0 to 7296
Outputs:
- fisher_band: bfloat16 [8192, 11392], P('subj', ('row', 'col')), parts along dimension 0
There are 2 independent parts, one for each index of `subj`. A program takes and returns all parts, laid end to end along the dimension named above; an argument that names none is the same for every part. Nothing has to cross between parts.
Inputs may be any that keep to these rules, and one draw needn't show every extreme that they name: `tap_count`: frames farther than this from the centre get no weight. Time block d holds frames d * 8 to (d + 1) * 8 - 1; only its first kept_frames[d] frames are kept. `band_start`: the 4096 band grayordinates lie inside the grid.
All inputs are finite; a program needn't handle non-finite values.
Results may differ from a plain program's by a relative error of at most 0.0031.
The roundings to bfloat16 on the way count: a program that leaves them out, or rounds other values in their place, can miss the bound.
Values may be sent and summed in bfloat16 or wider, within the bound.
No kernel may reach another device: no remote copies, remote signals or barrier semaphores. Data moves between devices by JAX's collectives and lax.ppermute only.
A program may use at most 128 MiB of HBM per device.

v0:
```python
import jax
import jax.numpy as jnp
from jax import lax
from jax.sharding import PartitionSpec as P

B = 4096
EPSILON = 1e-06
CLIP_LIMIT = 0.999


def with_halo(cells, sides, width):
    for axis, dim in sides:
        count = lax.axis_size(axis)
        ends = count - 1
        head = lax.slice_in_dim(cells, 0, width, axis=dim)
        tail = lax.slice_in_dim(cells, cells.shape[dim] - width, cells.shape[dim], axis=dim)
        cells = jnp.concatenate(
            [
                lax.ppermute(tail, axis, [(i, (i + 1) % count) for i in range(ends)]),
                cells,
                lax.ppermute(head, axis, [((i + 1) % count, i) for i in range(ends)]),
            ],
            axis=dim,
        )
    return cells


def tap_table(tap_values, tap_count):
    tap_reach = tap_values.shape[0] // 2
    offsets = jnp.arange(tap_values.shape[0], dtype=jnp.int32) - tap_reach
    active = (jnp.abs(offsets) <= tap_count[0]).astype(jnp.float32)
    centre = jnp.sum(active * tap_values) / jnp.sum(active)
    return active * (tap_values - centre)


def band_filter(padded, tap_weights, length):
    filtered = tap_weights[0] * padded[0:length]
    for tap_index in range(1, tap_weights.shape[0]):
        filtered = filtered + tap_weights[tap_index] * padded[tap_index : tap_index + length]
    return filtered


def fisher_z(correlation):
    clipped = jnp.clip(correlation, -CLIP_LIMIT, CLIP_LIMIT)
    return 0.5 * (jnp.log1p(clipped) - jnp.log1p(-clipped))


def body(series, tap_values, tap_count, kept_frames, band_start):
    tap_reach = tap_values.shape[0] // 2
    tap_weights = tap_table(tap_values, tap_count)
    block_len = series.shape[0]
    padded = with_halo(series, ((("row", "col"), 0),), tap_reach)
    filtered = band_filter(padded, tap_weights, block_len)
    own_kept = kept_frames[lax.axis_index(("row", "col"))]
    keep_mask = (jnp.arange(block_len, dtype=jnp.int32) < own_kept).astype(jnp.float32)[:, None]
    centered = keep_mask * filtered
    spread = lax.psum(jnp.sum(centered * centered, axis=0), ("row", "col"))
    scaled = (centered * lax.rsqrt(spread + EPSILON)).astype(jnp.bfloat16)
    columns = lax.all_to_all(scaled, ("row", "col"), split_axis=1, concat_axis=0, tiled=True)
    band_slice = lax.dynamic_slice_in_dim(scaled, band_start[0], B, 1)
    band_cols = lax.all_gather(band_slice, ("row", "col"), axis=0, tiled=True)
    correlation = lax.dot_general(
        band_cols, columns, (((0,), (0,)), ((), ())), preferred_element_type=jnp.float32
    )
    return fisher_z(correlation).astype(jnp.bfloat16)


def solution(mesh):
    placed = (P(("subj", "row", "col"), None), P(), P(), P("subj"), P("subj"))
    return jax.shard_map(
        body, mesh=mesh, in_specs=placed, out_specs=P("subj", ("row", "col")), check_vma=False
    )
```

profile of v0, /device:TPU:0, one launch (start us, length us, event | category | flops | bytes accessed | tf_op | source)
XLA Modules:
  0.0 151.6 jit_solution(5790544908060387476)
XLA Ops:
  6.5 0.0 all-gather.2.cloned.1.call-start
  6.5 2.4 %collective-permute-start = (f32[8,11392]{1,0:T(8,128)}, f32[8,11392]{1,0:T(8,128)S(1)}, u32[]{:S(2)}, u32[]{:S(2)}) collective-permute-start(f32[8,11392]{1,0:T(8,128)} %param.5), channel_id=1, source_target_pairs={{0,1},{1,2},{2,3},{3,4},{4,5},{5,6},{6,7},{7,8},{8,9},{9,10},{10,1... | collective-permute-start | bytes 1093640 | tf_op jit(solution)/shard_map/ppermute | solution.py:19
  8.9 1.3 collective-permute-start.1
  10.9 1.3 dynamic_slice.6
  12.1 1.3 convert_reduce_fusion
  13.5 0.6 compare_convert_fusion
  16.1 0.7 subtract_select_fusion
  16.7 0.7 fusion.19
  17.4 0.0 collective-permute-done
  17.5 1.0 constant_dynamic-update-slice_fusion
  18.5 0.0 collective-permute-done.1
  18.6 12.4 %multiply_reduce_fusion = (f32[11392]{0:T(1024)S(1)}, f32[8,11392]{1,0:T(8,128)S(1)}) fusion(f32[8,11392]{1,0:T(8,128)S(1)} %collective-permute-done.1, f32[]{:T(128)} %bitcast.18, f32[16,11392]{1,0:T(8,128)S(1)} %constant_dynamic-update-slice_fusion.2, f32[]{:T(128)} %bitcast.17, f32[]{:T(128)} %bitcast.16, f32[]{:T(128)} %bitcast.15, f32[]{:T(128)} %bitcast.14, ...), kind=kLoop, calls=%fused_computation.33 | loop fusion | flops 3269504 | bytes 6607460 | tf_op jit(solution)/shard_map/reduce_sum | solution.py:57
  31.0 63.9 %psum.7 = f32[11392]{0:T(1024)S(1)} all-reduce(f32[11392]{0:T(1024)S(1)} %get-tuple-element.5), channel_id=1, replica_groups=mesh['subj'=2,'row'=8,'col'=2] {'row','col'}, use_global_device_ids=true, to_apply=%region_3.0 | all-reduce | flops 11392 | bytes 91136 | tf_op jit(solution)/shard_map/psum | solution.py:57
  94.9 0.7 constant_dynamic-slice_fusion
  95.7 0.0 all-gather.2.cloned.1.call-update
  95.7 0.4 all_to_all.14
  96.1 0.1 copy.6
  96.2 12.3 %all_to_all.19 = bf16[8,16,712]{2,0,1:T(8,128)(2,1)S(1)} all-to-all(bf16[8,16,712]{2,0,1:T(8,128)(2,1)S(1)} %copy.6), channel_id=1, replica_groups=mesh['subj'=2,'row'=8,'col'=2] {'row','col'}, dimensions={1} | all-to-all | bytes 364544 | tf_op jit(solution)/shard_map/all_to_all | solution.py:59
  108.5 23.6 %all-gather.2.cloned.1.call-done = bf16[128,4096]{1,0:T(8,128)(2,1)} async-done(((bf16[8,4096]{1,0:T(8,128)(2,1)}), bf16[128,4096]{1,0:T(8,128)(2,1)}) %all-gather.2.cloned.1.call-update) | async-done | bytes 1048592 | tf_op jit(solution)/shard_map/all_gather | solution.py:61
  132.1 12.7 %multiply_convert_fusion = bf16[4096,712]{0,1:T(8,128)(2,1)} fusion(bf16[128,4096]{1,0:T(8,128)(2,1)} %all-gather.2.cloned.1.call-done, bf16[8,16,712]{2,0,1:T(8,128)(2,1)S(1)} %all_to_all.19), kind=kOutput, calls=%fused_computation | convolution fusion | flops 761167872 | bytes 7063552 | tf_op jit(solution)/shard_map/dot_general | solution.py:62
  (4 shorter events, 0.1 us)
Async XLA Ops:
  6.5 125.6 %all-gather.2.cloned.1.call-start = ((), (), s32[]{:S(2)}) async-start(), calls=%async_computation.1 | async-start | bytes 1114112 | tf_op jit(solution)/shard_map/all_gather | solution.py:61
  6.5 10.9 %collective-permute-start = (f32[8,11392]{1,0:T(8,128)}, f32[8,11392]{1,0:T(8,128)S(1)}, u32[]{:S(2)}, u32[]{:S(2)}) collective-permute-start(f32[8,11392]{1,0:T(8,128)} %param.5), channel_id=1, source_target_pairs={{0,1},{1,2},{2,3},{3,4},{4,5},{5,6},{6,7},{7,8},{8,9},{9,10},{10,1... | collective-permute-start | bytes 1093640 | tf_op jit(solution)/shard_map/ppermute | solution.py:19
  8.9 9.6 %collective-permute-start.1 = (f32[8,11392]{1,0:T(8,128)}, f32[8,11392]{1,0:T(8,128)S(1)}, u32[]{:S(2)}, u32[]{:S(2)}) collective-permute-start(f32[8,11392]{1,0:T(8,128)} %param.5), channel_id=1, source_target_pairs={{1,0},{2,1},{3,2},{4,3},{5,4},{6,5},{7,6},{8,7},{9,8},{10,9},{11,1... | collective-permute-start | bytes 1093640 | tf_op jit(solution)/shard_map/ppermute | solution.py:21
Sparse Core Ops, SparseCore 0:
  95.8 36.2 all-gather.1
where the time goes:
time: 152 us
  blocking collectives  76.2 us (50%)
  waiting for transfers between devices  23.6 us (16%)
  between operations  16.1 us (11%)
  other arithmetic  15.1 us (10%)
  matrix products  12.7 us (8%)
  local copies, waits for them, and re-layouts  4.28 us (3%)
  starting transfers between devices  3.66 us (2%)
    psum x1, blocking collectives, body(): spread = lax.psum(jnp.sum(centered * centered, axis=0), ('row', 'col'))  63.9 us
    all_gather x1, waiting for transfers between devices, body(): band_cols = lax.all_gather(band_slice, ('row', 'col'), axis=0, tiled=True)  23.6 us
    dot_general x1, matrix products, body(): lax.dot_general(band_cols, columns, (((0,), (0,)), ((), ())), preferred_e...  12.7 us
    reduce_sum x1, other arithmetic, body(): spread = lax.psum(jnp.sum(centered * centered, axis=0), ('row', 'col'))  12.4 us
    all_to_all x1, blocking collectives, body(): lax.all_to_all(scaled, ('row', 'col'), split_axis=1, concat_axis=0, tiled...  12.3 us
  transfers between devices with their start and end apart: 3, of which 1 were waited for; matrix products, arithmetic and copies ran while one was open for 4% of the time, Pallas kernels for 0%

commit v1 on v0

--- a/solution.py
+++ b/solution.py
@@ -2,10 +2,19 @@
 import jax.numpy as jnp
 from jax import lax
 from jax.sharding import PartitionSpec as P
+from jax.lax import axis_index, axis_size, ppermute
 
 B = 4096
 EPSILON = 1e-06
 CLIP_LIMIT = 0.999
+
+
+def link_the_axis_part(my_data, which_dim):
+    my_data = jnp.moveaxis(my_data, 0, which_dim)
+    new = my_data.shape
+    return my_data.reshape(
+        *new[:which_dim], new[which_dim] * new[which_dim + 1], *new[which_dim + 2 :]
+    )
 
 
 def with_halo(cells, sides, width):
@@ -58,7 +67,27 @@
     scaled = (centered * lax.rsqrt(spread + EPSILON)).astype(jnp.bfloat16)
     columns = lax.all_to_all(scaled, ("row", "col"), split_axis=1, concat_axis=0, tiled=True)
     band_slice = lax.dynamic_slice_in_dim(scaled, band_start[0], B, 1)
-    band_cols = lax.all_gather(band_slice, ("row", "col"), axis=0, tiled=True)
+
+    def list_the_node(frame, mesh_ax, axis_k):
+        axis_len = axis_size(mesh_ax)
+        stack_in = tuple(((i0, (i0 + 1) % axis_len) for i0 in range(axis_len)))
+        store = tuple(((to_i, at) for at, to_i in stack_in))
+        z1, mixed_arr = ([], [])
+        for h in range(axis_len - 1):
+            if h % 2 == 0:
+                z1.append(ppermute(z1[-1] if z1 else frame, axis_name=mesh_ax, perm=stack_in))
+            else:
+                mixed_arr.append(
+                    ppermute(mixed_arr[-1] if mixed_arr else frame, axis_name=mesh_ax, perm=store)
+                )
+        block_last = jnp.stack([*z1[::-1], frame, *mixed_arr], 0)
+        frame_out = axis_index(mesh_ax)
+        current_arr = len(z1)
+        even = frame_out - current_arr
+        block_last = block_last[(jnp.arange(axis_len) - even) % axis_len]
+        return link_the_axis_part(block_last, axis_k)
+
+    band_cols = list_the_node(band_slice, ("row", "col"), 0)
     correlation = lax.dot_general(
         band_cols, columns, (((0,), (0,)), ((), ())), preferred_element_type=jnp.float32
     )

time: 152 us -> 161 us (1.059)
  starting transfers between devices: 3.66 us -> 41 us
  between operations: 16.1 us -> 2.85 us
  blocking collectives: 76.2 us -> 63.9 us
  waiting for transfers between devices: 23.6 us -> 21.2 us
    ppermute x0 -> x15, starting transfers between devices: none -> 31.6 us  [the longest x7 31.5 us: list_the_node(): ppermute(mixed_arr[-1] if mixed_arr else frame, axis_name=mesh_ax, perm=s...]
    all_gather x1 -> x0, waiting for transfers between devices: 23.6 us -> none  [body(): band_cols = lax.all_gather(band_slice, ('row', 'col'), axis=0, tiled=True)]
    ppermute x0 -> x15, waiting for transfers between devices: none -> 19.4 us  [the longest x8 17.7 us: list_the_node(): ppermute(z1[-1] if z1 else frame, axis_name=mesh_ax, perm=stack_in)]
    all_to_all x1 -> x0, blocking collectives: 12.3 us -> none  [body(): lax.all_to_all(scaled, ('row', 'col'), split_axis=1, concat_axis=0, tiled...]
    all_to_all x0 -> x1, starting transfers between devices: none -> 5.82 us  [body(): lax.all_to_all(scaled, ('row', 'col'), split_axis=1, concat_axis=0, tiled...]
    all_to_all x0 -> x1, waiting for transfers between devices: none -> 1.84 us  [body(): lax.all_to_all(scaled, ('row', 'col'), split_axis=1, concat_axis=0, tiled...]
  transfers between devices with their start and end apart: 3 -> 18, of which waited for: 1 -> 9; matrix products, arithmetic and copies ran while one was open for 4% -> 4% of each run, Pallas kernels for 0% -> 0%
where the time goes in v1:
time: 161 us
  blocking collectives  63.9 us (40%)
  starting transfers between devices  41 us (25%)
  waiting for transfers between devices  21.2 us (13%)
  other arithmetic  15 us (9%)
  matrix products  11.5 us (7%)
  local copies, waits for them, and re-layouts  5.1 us (3%)
  between operations  2.85 us (2%)
    psum x1, blocking collectives, body(): spread = lax.psum(jnp.sum(centered * centered, axis=0), ('row', 'col'))  63.9 us
    ppermute x7, starting transfers between devices, list_the_node(): ppermute(mixed_arr[-1] if mixed_arr else frame, axis_name=mesh_ax, perm=s...  31.5 us
    ppermute x8, waiting for transfers between devices, list_the_node(): ppermute(z1[-1] if z1 else frame, axis_name=mesh_ax, perm=stack_in)  17.7 us
    reduce_sum x1, other arithmetic, body(): spread = lax.psum(jnp.sum(centered * centered, axis=0), ('row', 'col'))  12.4 us
    dot_general x1, matrix products, body(): lax.dot_general(band_cols, columns, (((0,), (0,)), ((), ())), preferred_e...  11.5 us
    all_to_all x1, starting transfers between devices, body(): lax.all_to_all(scaled, ('row', 'col'), split_axis=1, concat_axis=0, tiled...  5.82 us
  transfers between devices with their start and end apart: 18, of which 9 were waited for; matrix products, arithmetic and copies ran while one was open for 4% of the time, Pallas kernels for 0%

profile of v1, /device:TPU:0, one launch (start us, length us, event | category | flops | bytes accessed | tf_op | source)
XLA Modules:
  0.0 160.6 jit_solution(198182982425826788)
XLA Ops:
  0.0 2.4 %collective-permute-start = (f32[8,11392]{1,0:T(8,128)}, f32[8,11392]{1,0:T(8,128)S(1)}, u32[]{:S(2)}, u32[]{:S(2)}) collective-permute-start(f32[8,11392]{1,0:T(8,128)} %param.5), channel_id=1, source_target_pairs={{0,1},{1,2},{2,3},{3,4},{4,5},{5,6},{6,7},{7,8},{8,9},{9,10},{10,1... | collective-permute-start | bytes 1093640 | tf_op jit(solution)/shard_map/ppermute | solution.py:28
  2.4 1.3 collective-permute-start.1
  4.3 1.2 dynamic_slice.6
  5.6 1.3 convert_reduce_fusion
  6.9 0.6 compare_convert_fusion
  9.4 0.7 subtract_select_fusion
  10.1 0.7 fusion.21
  10.8 0.0 collective-permute-done
  10.8 1.0 constant_dynamic-update-slice_fusion
  11.9 0.0 collective-permute-done.1
  11.9 12.4 %multiply_reduce_fusion = (f32[11392]{0:T(1024)S(1)}, f32[8,11392]{1,0:T(8,128)S(1)}) fusion(f32[8,11392]{1,0:T(8,128)S(1)} %collective-permute-done.1, f32[]{:T(128)} %bitcast.18, f32[16,11392]{1,0:T(8,128)S(1)} %constant_dynamic-update-slice_fusion.2, f32[]{:T(128)} %bitcast.17, f32[]{:T(128)} %bitcast.16, f32[]{:T(128)} %bitcast.15, f32[]{:T(128)} %bitcast.14, ...), kind=kLoop, calls=%fused_computation.35 | loop fusion | flops 3269504 | bytes 6607460 | tf_op jit(solution)/shard_map/reduce_sum | solution.py:66
  24.3 63.9 %psum.7 = f32[11392]{0:T(1024)S(1)} all-reduce(f32[11392]{0:T(1024)S(1)} %get-tuple-element.5), channel_id=1, replica_groups=mesh['subj'=2,'row'=8,'col'=2] {'row','col'}, use_global_device_ids=true, to_apply=%region_3.0 | all-reduce | flops 11392 | bytes 91136 | tf_op jit(solution)/shard_map/psum | solution.py:66
  88.3 0.1 constant_dynamic-slice_fusion
  88.4 0.1 collective-permute-start.2
  88.5 6.4 %collective-permute-done.2 = bf16[8,4096]{1,0:T(8,128)(2,1)S(1)} collective-permute-done((bf16[8,4096]{1,0:T(8,128)(2,1)S(1)}, bf16[8,4096]{1,0:T(8,128)(2,1)S(1)}, u32[]{:S(2)}, u32[]{:S(2)}) %collective-permute-start.2) | collective-permute-done | bytes 65568 | tf_op jit(solution)/shard_map/ppermute | solution.py:78
  94.8 0.0 collective-permute-start.3
  94.8 4.4 %collective-permute-start.10 = (bf16[8,4096]{1,0:T(8,128)(2,1)S(1)}, bf16[8,4096]{1,0:T(8,128)(2,1)S(1)}, u32[]{:S(2)}, u32[]{:S(2)}) collective-permute-start(bf16[8,4096]{1,0:T(8,128)(2,1)S(1)} %constant_dynamic-slice_fusion), channel_id=1, source_target_pairs={{1,0},{2,1},{3,2},{4,3},{5,4},{6,5},{7,6},{8,7},{9,8},{10,9},{11,1... | collective-permute-start | bytes 196616 | tf_op jit(solution)/shard_map/ppermute | solution.py:81
  99.3 1.9 %collective-permute-done.3 = bf16[8,4096]{1,0:T(8,128)(2,1)S(1)} collective-permute-done((bf16[8,4096]{1,0:T(8,128)(2,1)S(1)}, bf16[8,4096]{1,0:T(8,128)(2,1)S(1)}, u32[]{:S(2)}, u32[]{:S(2)}) %collective-permute-start.3) | collective-permute-done | bytes 65568 | tf_op jit(solution)/shard_map/ppermute | solution.py:78
  101.2 0.0 collective-permute-start.4
  101.2 0.0 collective-permute-done.10
  101.2 4.5 %collective-permute-start.11 = (bf16[8,4096]{1,0:T(8,128)(2,1)S(1)}, bf16[8,4096]{1,0:T(8,128)(2,1)S(1)}, u32[]{:S(2)}, u32[]{:S(2)}) collective-permute-start(bf16[8,4096]{1,0:T(8,128)(2,1)S(1)} %collective-permute-done.10), channel_id=1, source_target_pairs={{1,0},{2,1},{3,2},{4,3},{5,4},{6,5},{7,6},{8,7},{9,8},{10,9},{11,1... | collective-permute-start | bytes 196616 | tf_op jit(solution)/shard_map/ppermute | solution.py:81
  105.7 1.9 %collective-permute-done.4 = bf16[8,4096]{1,0:T(8,128)(2,1)S(1)} collective-permute-done((bf16[8,4096]{1,0:T(8,128)(2,1)S(1)}, bf16[8,4096]{1,0:T(8,128)(2,1)S(1)}, u32[]{:S(2)}, u32[]{:S(2)}) %collective-permute-start.4) | collective-permute-done | bytes 65568 | tf_op jit(solution)/shard_map/ppermute | solution.py:78
  107.6 0.0 collective-permute-start.5
  107.6 0.0 collective-permute-done.11
  107.6 4.5 %collective-permute-start.12 = (bf16[8,4096]{1,0:T(8,128)(2,1)S(1)}, bf16[8,4096]{1,0:T(8,128)(2,1)S(1)}, u32[]{:S(2)}, u32[]{:S(2)}) collective-permute-start(bf16[8,4096]{1,0:T(8,128)(2,1)S(1)} %collective-permute-done.11), channel_id=1, source_target_pairs={{1,0},{2,1},{3,2},{4,3},{5,4},{6,5},{7,6},{8,7},{9,8},{10,9},{11,1... | collective-permute-start | bytes 196616 | tf_op jit(solution)/shard_map/ppermute | solution.py:81
  112.1 1.9 %collective-permute-done.5 = bf16[8,4096]{1,0:T(8,128)(2,1)S(1)} collective-permute-done((bf16[8,4096]{1,0:T(8,128)(2,1)S(1)}, bf16[8,4096]{1,0:T(8,128)(2,1)S(1)}, u32[]{:S(2)}, u32[]{:S(2)}) %collective-permute-start.5) | collective-permute-done | bytes 65568 | tf_op jit(solution)/shard_map/ppermute | solution.py:78
  114.0 0.0 collective-permute-start.6
  114.0 0.0 collective-permute-done.12
  114.0 4.5 %collective-permute-start.13 = (bf16[8,4096]{1,0:T(8,128)(2,1)S(1)}, bf16[8,4096]{1,0:T(8,128)(2,1)S(1)}, u32[]{:S(2)}, u32[]{:S(2)}) collective-permute-start(bf16[8,4096]{1,0:T(8,128)(2,1)S(1)} %collective-permute-done.12), channel_id=1, source_target_pairs={{1,0},{2,1},{3,2},{4,3},{5,4},{6,5},{7,6},{8,7},{9,8},{10,9},{11,1... | collective-permute-start | bytes 196616 | tf_op jit(solution)/shard_map/ppermute | solution.py:81
  118.5 1.9 %collective-permute-done.6 = bf16[8,4096]{1,0:T(8,128)(2,1)S(1)} collective-permute-done((bf16[8,4096]{1,0:T(8,128)(2,1)S(1)}, bf16[8,4096]{1,0:T(8,128)(2,1)S(1)}, u32[]{:S(2)}, u32[]{:S(2)}) %collective-permute-start.6) | collective-permute-done | bytes 65568 | tf_op jit(solution)/shard_map/ppermute | solution.py:78
  120.4 0.0 collective-permute-start.7
  120.4 0.0 collective-permute-done.13
  120.4 4.5 %collective-permute-start.14 = (bf16[8,4096]{1,0:T(8,128)(2,1)S(1)}, bf16[8,4096]{1,0:T(8,128)(2,1)S(1)}, u32[]{:S(2)}, u32[]{:S(2)}) collective-permute-start(bf16[8,4096]{1,0:T(8,128)(2,1)S(1)} %collective-permute-done.13), channel_id=1, source_target_pairs={{1,0},{2,1},{3,2},{4,3},{5,4},{6,5},{7,6},{8,7},{9,8},{10,9},{11,1... | collective-permute-start | bytes 196616 | tf_op jit(solution)/shard_map/ppermute | solution.py:81
  124.9 1.9 %collective-permute-done.7 = bf16[8,4096]{1,0:T(8,128)(2,1)S(1)} collective-permute-done((bf16[8,4096]{1,0:T(8,128)(2,1)S(1)}, bf16[8,4096]{1,0:T(8,128)(2,1)S(1)}, u32[]{:S(2)}, u32[]{:S(2)}) %collective-permute-start.7) | collective-permute-done | bytes 65568 | tf_op jit(solution)/shard_map/ppermute | solution.py:78
  126.8 0.0 collective-permute-done.14
  126.8 4.5 %collective-permute-start.15 = (bf16[8,4096]{1,0:T(8,128)(2,1)S(1)}, bf16[8,4096]{1,0:T(8,128)(2,1)S(1)}, u32[]{:S(2)}, u32[]{:S(2)}) collective-permute-start(bf16[8,4096]{1,0:T(8,128)(2,1)S(1)} %collective-permute-done.14), channel_id=1, source_target_pairs={{1,0},{2,1},{3,2},{4,3},{5,4},{6,5},{7,6},{8,7},{9,8},{10,9},{11,1... | collective-permute-start | bytes 196616 | tf_op jit(solution)/shard_map/ppermute | solution.py:81
  131.3 1.9 %collective-permute-done.8 = bf16[8,4096]{1,0:T(8,128)(2,1)S(1)} collective-permute-done((bf16[8,4096]{1,0:T(8,128)(2,1)S(1)}, bf16[8,4096]{1,0:T(8,128)(2,1)S(1)}, u32[]{:S(2)}, u32[]{:S(2)}) %collective-permute-start.8) | collective-permute-done | bytes 65568 | tf_op jit(solution)/shard_map/ppermute | solution.py:78
  133.2 0.0 collective-permute-start.9
  133.2 0.4 all_to_all.12
  133.6 0.7 copy.9
  134.3 5.8 %all-to-all-start = ((bf16[8,16,712]{2,0,1:T(8,128)(2,1)}), bf16[8,16,712]{2,0,1:T(8,128)(2,1)S(1)}, u32[]{:S(2)}, u32[]{:S(2)}) async-start(bf16[8,16,712]{2,0,1:T(8,128)(2,1)} %copy.9), calls=%async_computation | async-start | bytes 393216 | tf_op jit(solution)/shard_map/all_to_all | solution.py:68
  140.2 4.6 %collective-permute-start.16 = (bf16[8,4096]{1,0:T(8,128)(2,1)S(1)}, bf16[8,4096]{1,0:T(8,128)(2,1)S(1)}, u32[]{:S(2)}, u32[]{:S(2)}) collective-permute-start(bf16[8,4096]{1,0:T(8,128)(2,1)S(1)} %collective-permute-done.15), channel_id=1, source_target_pairs={{1,0},{2,1},{3,2},{4,3},{5,4},{6,5},{7,6},{8,7},{9,8},{10,9},{11,1... | collective-permute-start | bytes 196616 | tf_op jit(solution)/shard_map/ppermute | solution.py:81
  144.8 0.0 collective-permute-done.9
  144.9 0.1 bitcast_dynamic-update-slice_fusion.7
  145.1 1.6 collective-permute-done.16
  146.7 0.6 gather_fusion
  147.3 1.8 %all-to-all-done = bf16[8,16,712]{2,0,1:T(8,128)(2,1)S(1)} async-done(((bf16[8,16,712]{2,0,1:T(8,128)(2,1)}), bf16[8,16,712]{2,0,1:T(8,128)(2,1)S(1)}, u32[]{:S(2)}, u32[]{:S(2)}) %all-to-all-start) | async-done | bytes 182304 | tf_op jit(solution)/shard_map/all_to_all | solution.py:68
  149.2 11.5 %multiply_convert_fusion = bf16[4096,712]{0,1:T(8,128)(2,1)} fusion(bf16[16,8,4096]{2,1,0:T(8,128)(2,1)S(1)} %gather_fusion, bf16[8,16,712]{2,0,1:T(8,128)(2,1)S(1)} %all-to-all-done), kind=kOutput, calls=%fused_computation.2 | convolution fusion | flops 761167872 | bytes 7063552 | tf_op jit(solution)/shard_map/dot_general | solution.py:91
  (23 shorter events, 0.2 us)
Async XLA Ops:
  0.0 10.8 %collective-permute-start = (f32[8,11392]{1,0:T(8,128)}, f32[8,11392]{1,0:T(8,128)S(1)}, u32[]{:S(2)}, u32[]{:S(2)}) collective-permute-start(f32[8,11392]{1,0:T(8,128)} %param.5), channel_id=1, source_target_pairs={{0,1},{1,2},{2,3},{3,4},{4,5},{5,6},{6,7},{7,8},{8,9},{9,10},{10,1... | collective-permute-start | bytes 1093640 | tf_op jit(solution)/shard_map/ppermute | solution.py:28
  2.4 9.5 %collective-permute-start.1 = (f32[8,11392]{1,0:T(8,128)}, f32[8,11392]{1,0:T(8,128)S(1)}, u32[]{:S(2)}, u32[]{:S(2)}) collective-permute-start(f32[8,11392]{1,0:T(8,128)} %param.5), channel_id=1, source_target_pairs={{1,0},{2,1},{3,2},{4,3},{5,4},{6,5},{7,6},{8,7},{9,8},{10,9},{11,1... | collective-permute-start | bytes 1093640 | tf_op jit(solution)/shard_map/ppermute | solution.py:30
  88.4 6.4 %collective-permute-start.2 = (bf16[8,4096]{1,0:T(8,128)(2,1)S(1)}, bf16[8,4096]{1,0:T(8,128)(2,1)S(1)}, u32[]{:S(2)}, u32[]{:S(2)}) collective-permute-start(bf16[8,4096]{1,0:T(8,128)(2,1)S(1)} %constant_dynamic-slice_fusion), channel_id=1, source_target_pairs={{0,1},{1,2},{2,3},{3,4},{4,5},{5,6},{6,7},{7,8},{8,9},{9,10},{10,1... | collective-permute-start | bytes 196616 | tf_op jit(solution)/shard_map/ppermute | solution.py:78
  94.8 6.4 %collective-permute-start.3 = (bf16[8,4096]{1,0:T(8,128)(2,1)S(1)}, bf16[8,4096]{1,0:T(8,128)(2,1)S(1)}, u32[]{:S(2)}, u32[]{:S(2)}) collective-permute-start(bf16[8,4096]{1,0:T(8,128)(2,1)S(1)} %collective-permute-done.2), channel_id=1, source_target_pairs={{0,1},{1,2},{2,3},{3,4},{4,5},{5,6},{6,7},{7,8},{8,9},{9,10},{10,1... | collective-permute-start | bytes 196616 | tf_op jit(solution)/shard_map/ppermute | solution.py:78
  94.8 6.4 %collective-permute-start.10 = (bf16[8,4096]{1,0:T(8,128)(2,1)S(1)}, bf16[8,4096]{1,0:T(8,128)(2,1)S(1)}, u32[]{:S(2)}, u32[]{:S(2)}) collective-permute-start(bf16[8,4096]{1,0:T(8,128)(2,1)S(1)} %constant_dynamic-slice_fusion), channel_id=1, source_target_pairs={{1,0},{2,1},{3,2},{4,3},{5,4},{6,5},{7,6},{8,7},{9,8},{10,9},{11,1... | collective-permute-start | bytes 196616 | tf_op jit(solution)/shard_map/ppermute | solution.py:81
  101.2 6.4 %collective-permute-start.4 = (bf16[8,4096]{1,0:T(8,128)(2,1)S(1)}, bf16[8,4096]{1,0:T(8,128)(2,1)S(1)}, u32[]{:S(2)}, u32[]{:S(2)}) collective-permute-start(bf16[8,4096]{1,0:T(8,128)(2,1)S(1)} %collective-permute-done.3), channel_id=1, source_target_pairs={{0,1},{1,2},{2,3},{3,4},{4,5},{5,6},{6,7},{7,8},{8,9},{9,10},{10,1... | collective-permute-start | bytes 196616 | tf_op jit(solution)/shard_map/ppermute | solution.py:78
  101.2 6.4 %collective-permute-start.11 = (bf16[8,4096]{1,0:T(8,128)(2,1)S(1)}, bf16[8,4096]{1,0:T(8,128)(2,1)S(1)}, u32[]{:S(2)}, u32[]{:S(2)}) collective-permute-start(bf16[8,4096]{1,0:T(8,128)(2,1)S(1)} %collective-permute-done.10), channel_id=1, source_target_pairs={{1,0},{2,1},{3,2},{4,3},{5,4},{6,5},{7,6},{8,7},{9,8},{10,9},{11,1... | collective-permute-start | bytes 196616 | tf_op jit(solution)/shard_map/ppermute | solution.py:81
  107.6 6.4 %collective-permute-start.5 = (bf16[8,4096]{1,0:T(8,128)(2,1)S(1)}, bf16[8,4096]{1,0:T(8,128)(2,1)S(1)}, u32[]{:S(2)}, u32[]{:S(2)}) collective-permute-start(bf16[8,4096]{1,0:T(8,128)(2,1)S(1)} %collective-permute-done.4), channel_id=1, source_target_pairs={{0,1},{1,2},{2,3},{3,4},{4,5},{5,6},{6,7},{7,8},{8,9},{9,10},{10,1... | collective-permute-start | bytes 196616 | tf_op jit(solution)/shard_map/ppermute | solution.py:78
  107.6 6.4 %collective-permute-start.12 = (bf16[8,4096]{1,0:T(8,128)(2,1)S(1)}, bf16[8,4096]{1,0:T(8,128)(2,1)S(1)}, u32[]{:S(2)}, u32[]{:S(2)}) collective-permute-start(bf16[8,4096]{1,0:T(8,128)(2,1)S(1)} %collective-permute-done.11), channel_id=1, source_target_pairs={{1,0},{2,1},{3,2},{4,3},{5,4},{6,5},{7,6},{8,7},{9,8},{10,9},{11,1... | collective-permute-start | bytes 196616 | tf_op jit(solution)/shard_map/ppermute | solution.py:81
  114.0 6.4 %collective-permute-start.6 = (bf16[8,4096]{1,0:T(8,128)(2,1)S(1)}, bf16[8,4096]{1,0:T(8,128)(2,1)S(1)}, u32[]{:S(2)}, u32[]{:S(2)}) collective-permute-start(bf16[8,4096]{1,0:T(8,128)(2,1)S(1)} %collective-permute-done.5), channel_id=1, source_target_pairs={{0,1},{1,2},{2,3},{3,4},{4,5},{5,6},{6,7},{7,8},{8,9},{9,10},{10,1... | collective-permute-start | bytes 196616 | tf_op jit(solution)/shard_map/ppermute | solution.py:78
  114.0 6.4 %collective-permute-start.13 = (bf16[8,4096]{1,0:T(8,128)(2,1)S(1)}, bf16[8,4096]{1,0:T(8,128)(2,1)S(1)}, u32[]{:S(2)}, u32[]{:S(2)}) collective-permute-start(bf16[8,4096]{1,0:T(8,128)(2,1)S(1)} %collective-permute-done.12), channel_id=1, source_target_pairs={{1,0},{2,1},{3,2},{4,3},{5,4},{6,5},{7,6},{8,7},{9,8},{10,9},{11,1... | collective-permute-start | bytes 196616 | tf_op jit(solution)/shard_map/ppermute | solution.py:81
  120.4 6.4 %collective-permute-start.7 = (bf16[8,4096]{1,0:T(8,128)(2,1)S(1)}, bf16[8,4096]{1,0:T(8,128)(2,1)S(1)}, u32[]{:S(2)}, u32[]{:S(2)}) collective-permute-start(bf16[8,4096]{1,0:T(8,128)(2,1)S(1)} %collective-permute-done.6), channel_id=1, source_target_pairs={{0,1},{1,2},{2,3},{3,4},{4,5},{5,6},{6,7},{7,8},{8,9},{9,10},{10,1... | collective-permute-start | bytes 196616 | tf_op jit(solution)/shard_map/ppermute | solution.py:78
  120.4 6.4 %collective-permute-start.14 = (bf16[8,4096]{1,0:T(8,128)(2,1)S(1)}, bf16[8,4096]{1,0:T(8,128)(2,1)S(1)}, u32[]{:S(2)}, u32[]{:S(2)}) collective-permute-start(bf16[8,4096]{1,0:T(8,128)(2,1)S(1)} %collective-permute-done.13), channel_id=1, source_target_pairs={{1,0},{2,1},{3,2},{4,3},{5,4},{6,5},{7,6},{8,7},{9,8},{10,9},{11,1... | collective-permute-start | bytes 196616 | tf_op jit(solution)/shard_map/ppermute | solution.py:81
  126.8 6.4 %collective-permute-start.8 = (bf16[8,4096]{1,0:T(8,128)(2,1)S(1)}, bf16[8,4096]{1,0:T(8,128)(2,1)S(1)}, u32[]{:S(2)}, u32[]{:S(2)}) collective-permute-start(bf16[8,4096]{1,0:T(8,128)(2,1)S(1)} %collective-permute-done.7), channel_id=1, source_target_pairs={{0,1},{1,2},{2,3},{3,4},{4,5},{5,6},{6,7},{7,8},{8,9},{9,10},{10,1... | collective-permute-start | bytes 196616 | tf_op jit(solution)/shard_map/ppermute | solution.py:78
  126.8 13.4 %collective-permute-start.15 = (bf16[8,4096]{1,0:T(8,128)(2,1)S(1)}, bf16[8,4096]{1,0:T(8,128)(2,1)S(1)}, u32[]{:S(2)}, u32[]{:S(2)}) collective-permute-start(bf16[8,4096]{1,0:T(8,128)(2,1)S(1)} %collective-permute-done.14), channel_id=1, source_target_pairs={{1,0},{2,1},{3,2},{4,3},{5,4},{6,5},{7,6},{8,7},{9,8},{10,9},{11,1... | collective-permute-start | bytes 196616 | tf_op jit(solution)/shard_map/ppermute | solution.py:81
  133.2 11.6 %collective-permute-start.9 = (bf16[8,4096]{1,0:T(8,128)(2,1)S(1)}, bf16[8,4096]{1,0:T(8,128)(2,1)S(1)}, u32[]{:S(2)}, u32[]{:S(2)}) collective-permute-start(bf16[8,4096]{1,0:T(8,128)(2,1)S(1)} %collective-permute-done.8), channel_id=1, source_target_pairs={{0,1},{1,2},{2,3},{3,4},{4,5},{5,6},{6,7},{7,8},{8,9},{9,10},{10,1... | collective-permute-start | bytes 196616 | tf_op jit(solution)/shard_map/ppermute | solution.py:78
  134.3 14.8 %all-to-all-start = ((bf16[8,16,712]{2,0,1:T(8,128)(2,1)}), bf16[8,16,712]{2,0,1:T(8,128)(2,1)S(1)}, u32[]{:S(2)}, u32[]{:S(2)}) async-start(bf16[8,16,712]{2,0,1:T(8,128)(2,1)} %copy.9), calls=%async_computation | async-start | bytes 393216 | tf_op jit(solution)/shard_map/all_to_all | solution.py:68
  140.2 6.5 %collective-permute-start.16 = (bf16[8,4096]{1,0:T(8,128)(2,1)S(1)}, bf16[8,4096]{1,0:T(8,128)(2,1)S(1)}, u32[]{:S(2)}, u32[]{:S(2)}) collective-permute-start(bf16[8,4096]{1,0:T(8,128)(2,1)S(1)} %collective-permute-done.15), channel_id=1, source_target_pairs={{1,0},{2,1},{3,2},{4,3},{5,4},{6,5},{7,6},{8,7},{9,8},{10,9},{11,1... | collective-permute-start | bytes 196616 | tf_op jit(solution)/shard_map/ppermute | solution.py:81
